TPU v7x, 256 devices: a whole 4x4x8 slice. The times are simulated.
256 devices in a mesh: section: 16 (over z_lo, y), dp: 16 (over x, z_hi, core).
Axes of the slice: x: 4, y: 4, z: 8 (z_hi: 2, z_lo: 4; z = z_hi * 4 + z_lo), core: 2. Of those that a mesh axis runs over, the one named last changes fastest.
Arguments:
- enc_state: bfloat16 [16, 512, 4096], P('section', 'dp'), may hold values from -1000 to 1000
- final_gain: float32 [4096], replicated, may hold values from 0.5 to 1.5
- queries: bfloat16 [16, 2048, 4096], P('section', 'dp'), may hold values from -60 to 60
- w_key: bfloat16 [16, 4096, 4096], P('section', None, 'dp'), may hold values from -0.09375 to 0.09375
- w_value: bfloat16 [16, 4096, 4096], P('section', None, 'dp'), may hold values from -0.09375 to 0.09375
- ctx_grad: bfloat16 [16, 2048, 4096], P('section', 'dp'), may hold values from -6 to 6
- mem_len: int32 [16], P('dp'), may hold values from 8 to 32, as said below
Outputs:
- query_grad: bfloat16 [16, 2048, 4096], P('section', 'dp')
- key_weight_grad: bfloat16 [16, 4096, 4096], P('section', None, 'dp')
- value_weight_grad: bfloat16 [16, 4096, 4096], P('section', None, 'dp')
- state_grad: bfloat16 [16, 512, 4096], P('section', 'dp')
- gain_grad: float32 [4096], replicated
Inputs may be any that keep to these rules, and one draw needn't show every extreme that they name: Sequence b's memory holds mem_len[b] valid tokens from position 0; in every draw some sequence has all 32.
All inputs are finite; a program needn't handle non-finite values.
Results may differ from a plain program's by a relative error of at most 0.028.
The roundings to bfloat16 on the way count: a program that leaves them out, or rounds other values in their place, can miss the bound.
Values may be sent and summed in bfloat16 or wider, within the bound.
A program may use at most 64 MiB of HBM per device.

v0:
```python
import jax
import jax.numpy as jnp
from jax import lax
from jax.sharding import PartitionSpec as P

HEAD_DIM = 256
epsilon = 1e-06


def broadcast(block, axis, holder):
    block = jnp.where(lax.axis_index(axis) == holder, block, jnp.zeros_like(block))
    return lax.psum(block, axis)


def on_device(enc_state, final_gain, queries, w_key, w_value, ctx_grad, mem_len):
    sections = lax.axis_size("section")
    replicas = lax.axis_size("dp")
    section_index = lax.axis_index("section")
    last_encoder = sections // 2 - 1
    is_decoder = (section_index > last_encoder).astype(jnp.float32)
    is_last = (section_index == last_encoder).astype(jnp.float32)
    src_len = enc_state.shape[1]
    tgt_len = queries.shape[1]
    local_width = w_key.shape[2]
    heads_here = local_width // HEAD_DIM
    score_scale = HEAD_DIM ** (-0.5)
    enc_rows = enc_state[0].astype(jnp.float32)
    inverse = lax.rsqrt(jnp.mean(enc_rows * enc_rows, axis=1, keepdims=True) + epsilon)
    normed = enc_rows * inverse
    memory = (normed * final_gain).astype(jnp.bfloat16)
    sent = broadcast(memory, "section", last_encoder)
    all_memory, all_len = (
        lax.all_gather(sent, "dp", axis=0, tiled=True),
        lax.all_gather(mem_len, "dp", axis=0, tiled=True),
    )
    w_both = jnp.concatenate([w_key[0], w_value[0]], axis=1)
    projected = jnp.dot(all_memory, w_both, preferred_element_type=jnp.float32).astype(jnp.bfloat16)
    key_rows = projected[:, :local_width].reshape(replicas, src_len, heads_here, HEAD_DIM)
    value_rows = projected[:, local_width:].reshape(replicas, src_len, heads_here, HEAD_DIM)
    query_heads, grad_heads = (
        lax.all_to_all(queries[0], "dp", split_axis=1, concat_axis=0, tiled=True),
        lax.all_to_all(ctx_grad[0], "dp", split_axis=1, concat_axis=0, tiled=True),
    )
    query_rows = query_heads.reshape(replicas, tgt_len, heads_here, HEAD_DIM)
    grad_rows = grad_heads.reshape(replicas, tgt_len, heads_here, HEAD_DIM)
    key_valid = jnp.arange(src_len, dtype=jnp.int32)[None, :] < all_len[:, None]
    scores = (
        jnp.einsum("btha,buha->bhut", query_rows, key_rows, preferred_element_type=jnp.float32)
        * score_scale
    )
    scores = jnp.where(key_valid[:, None, :, None], scores, -1e30)
    row_max = jnp.max(scores, axis=2, keepdims=True)
    exponent = jnp.exp(scores - row_max)
    probs = exponent / jnp.sum(exponent, axis=2, keepdims=True)
    probs_low = probs.astype(jnp.bfloat16)
    grad_probs = jnp.einsum(
        "btha,buha->bhut", grad_rows, value_rows, preferred_element_type=jnp.float32
    )
    row_delta = jnp.sum(probs * grad_probs, axis=2, keepdims=True)
    grad_scores = (probs * (grad_probs - row_delta) * score_scale).astype(jnp.bfloat16)
    query_grad_heads = (
        jnp.einsum("bhut,buha->btha", grad_scores, key_rows, preferred_element_type=jnp.float32)
        .astype(jnp.bfloat16)
        .reshape(replicas * tgt_len, local_width)
    )
    key_grad = (
        jnp.einsum("bhut,btha->buha", grad_scores, query_rows, preferred_element_type=jnp.float32)
        .astype(jnp.bfloat16)
        .reshape(replicas * src_len, local_width)
    )
    value_grad = (
        jnp.einsum("bhut,btha->buha", probs_low, grad_rows, preferred_element_type=jnp.float32)
        .astype(jnp.bfloat16)
        .reshape(replicas * src_len, local_width)
    )
    both_grads = jnp.concatenate([key_grad, value_grad], axis=1)
    weight_grads = (
        lax.dot_general(
            all_memory, both_grads, (((0,), (0,)), ((), ())), preferred_element_type=jnp.float32
        )
        * is_decoder
    ).astype(jnp.bfloat16)
    query_back = lax.all_to_all(query_grad_heads, "dp", split_axis=0, concat_axis=1, tiled=True)
    query_grad = (query_back.astype(jnp.float32) * is_decoder).astype(jnp.bfloat16)[None]
    section_part = lax.psum_scatter(
        (
            lax.dot_general(
                both_grads, w_both, (((1,), (1,)), ((), ())), preferred_element_type=jnp.float32
            )
            * is_decoder
        ).astype(jnp.bfloat16),
        "dp",
        scatter_dimension=0,
        tiled=True,
    )
    memory_grad = lax.psum(section_part, "section").astype(jnp.float32)
    scaled_grad = memory_grad * final_gain
    last_grad = inverse * (
        scaled_grad - normed * jnp.mean(scaled_grad * normed, axis=1, keepdims=True)
    )
    state_grad = (last_grad * is_last).astype(jnp.bfloat16)[None]
    gain_grad = lax.psum(jnp.sum(memory_grad * normed, axis=0) * is_last, ("section", "dp"))
    key_weight_grad = weight_grads[:, :local_width][None]
    value_weight_grad = weight_grads[:, local_width:][None]
    return (query_grad, key_weight_grad, value_weight_grad, state_grad, gain_grad)


def solution(mesh):
    placed = (
        P("section", "dp", None),
        P(),
        P("section", "dp", None),
        P("section", None, "dp"),
        P("section", None, "dp"),
        P("section", "dp", None),
        P("dp"),
    )
    return jax.shard_map(
        on_device,
        mesh=mesh,
        in_specs=placed,
        out_specs=(
            P("section", "dp", None),
            P("section", None, "dp"),
            P("section", None, "dp"),
            P("section", "dp", None),
            P(),
        ),
        check_vma=False,
    )
```

profile of v0, /device:TPU:1, one launch (start us, length us, event | category | flops | bytes accessed | tf_op | source)
XLA Modules:
  0.0 639.9 jit_solution(12333519288310503521)
XLA Ops:
  7.2 1.2 fusion.28
  8.4 1.8 fusion.33
  10.3 156.1 %all-reduce.4.cloned.1.call-done = bf16[32,4096]{1,0:T(8,128)(2,1)} async-done(((bf16[32,4096]{1,0:T(8,128)(2,1)}), bf16[32,4096]{1,0:T(8,128)(2,1)}) %all-reduce.4.cloned.1.call-update) | async-done | bytes 262160 | tf_op jit(solution)/shard_map/psum | solution.py:12
  166.4 1.6 copy.13
  168.0 1.3 copy.14
  169.3 19.1 %all-to-all-start = ((bf16[128,16,256]{2,0,1:T(8,128)(2,1)}), bf16[128,16,256]{2,0,1:T(8,128)(2,1)S(1)}, u32[]{:S(2)}, u32[]{:S(2)}) async-start(bf16[128,16,256]{2,0,1:T(8,128)(2,1)} %copy.14), calls=%async_computation | async-start | bytes 2097152 | tf_op jit(solution)/shard_map/all_to_all | solution.py:41
  188.4 0.7 copy.15
  189.1 1.3 copy.16
  190.4 26.1 %all-to-all-done = bf16[128,16,256]{2,0,1:T(8,128)(2,1)S(1)} async-done(((bf16[128,16,256]{2,0,1:T(8,128)(2,1)}), bf16[128,16,256]{2,0,1:T(8,128)(2,1)S(1)}, u32[]{:S(2)}, u32[]{:S(2)}) %all-to-all-start) | async-done | bytes 1048608 | tf_op jit(solution)/shard_map/all_to_all | solution.py:41
  216.5 7.5 %all-to-all-start.1 = ((bf16[128,16,256]{2,0,1:T(8,128)(2,1)}), bf16[128,16,256]{2,0,1:T(8,128)(2,1)S(1)}, u32[]{:S(2)}, u32[]{:S(2)}) async-start(bf16[128,16,256]{2,0,1:T(8,128)(2,1)} %copy.16), calls=%async_computation.1 | async-start | bytes 2097152 | tf_op jit(solution)/shard_map/all_to_all | solution.py:42
  224.7 0.6 dynamic-slice
  225.3 0.8 dynamic-update-slice
  226.0 33.3 %all-reduce = s32[16]{0:T(128)S(1)} all-reduce(s32[16]{0:T(128)S(1)} %dynamic-update-slice), channel_id=1, replica_groups=mesh['section'=16,'dp'=16] {'dp'}, use_global_device_ids=true, to_apply=%add | all-reduce | flops 16 | bytes 128
  259.4 15.6 %all-gather.2.cloned.1.call-done = bf16[512,4096]{1,0:T(8,128)(2,1)} async-done(((bf16[32,4096]{1,0:T(8,128)(2,1)}), bf16[512,4096]{1,0:T(8,128)(2,1)}) %all-gather.2.cloned.1.call-update) | async-done | bytes 4194320 | tf_op jit(solution)/shard_map/all_gather | solution.py:33
  275.0 5.8 fusion.4
  280.8 0.5 fusion.10
  281.3 0.6 fusion.46
  281.9 0.5 fusion.13
  282.4 0.3 convolution_convert_fusion.1
  282.7 0.3 convolution_convert_fusion.2
  283.0 6.6 %multiply_convert_fusion = bf16[512,4096]{1,0:T(8,128)(2,1)} fusion(f32[]{:T(128)S(6)} %convert_element_type.108, bf16[4096,256]{1,0:T(8,128)(2,1)} %bitcast.67, bf16[4096,256]{1,0:T(8,128)(2,1)} %bitcast.69, bf16[512,256]{1,0:T(8,128)(2,1)S(1)} %bitcast.70, bf16[512,256]{1,0:T(8,128)(2,1)S(1)} %bitcast.72), kind=kOutput, calls=%fused_computation.2 | convolution fusion | flops 2161115136 | bytes 8912900 | tf_op jit(solution)/shard_map/dot_general | solution.py:87
  289.6 1.5 fusion.3
  291.1 3.7 all-to-all-start.2
  294.8 4.6 multiply_convert_fusion.1
  299.4 2.3 slice_bitcast_fusion
  301.7 91.4 %reduce-scatter.2.cloned.1.call-done = bf16[32,4096]{1,0:T(8,128)(2,1)} async-done(((bf16[512,4096]{1,0:T(8,128)(2,1)}), bf16[32,4096]{1,0:T(8,128)(2,1)}) %reduce-scatter.2.cloned.1.call-update) | async-done | bytes 262160 | tf_op jit(solution)/shard_map/reduce_scatter | solution.py:85
  393.2 0.3 multiply_convert_fusion.2
  393.5 1.3 copy.17
  394.8 150.1 %all-reduce.6.cloned.1.call-done = bf16[32,4096]{1,0:T(8,128)(2,1)} async-done(((bf16[32,4096]{1,0:T(8,128)(2,1)}), bf16[32,4096]{1,0:T(8,128)(2,1)}) %all-reduce.6.cloned.1.call-update) | async-done | bytes 262160 | tf_op jit(solution)/shard_map/psum | solution.py:96
  544.9 1.3 fusion.27
  546.2 85.3 %psum.23 = f32[4096]{0:T(1024)} all-reduce(f32[4096]{0:T(1024)S(1)} %broadcast_multiply_fusion), channel_id=1, replica_groups=mesh['section'=16,'dp'=16] {'section','dp'}, use_global_device_ids=true, to_apply=%region_9.10 | all-reduce | flops 4096 | bytes 32768 | tf_op jit(solution)/shard_map/psum | solution.py:102
  631.5 1.8 fusion.34
  (24 shorter events, 0.4 us)
Async XLA Ops:
  7.2 181.2 %copy-start.1 = (bf16[1,128,4096]{2,1,0:T(8,128)(2,1)S(1)}, bf16[1,128,4096]{2,1,0:T(8,128)(2,1)}, u32[]{:S(2)}) copy-start(bf16[1,128,4096]{2,1,0:T(8,128)(2,1)} %param.12) | copy-start | bytes 3145732
  7.2 159.2 %all-reduce.4.cloned.1.call-start = ((), (), s32[]{:S(2)}) async-start(), calls=%async_computation.4 | async-start | bytes 524288 | tf_op jit(solution)/shard_map/psum | solution.py:12
  10.3 264.7 %all-gather.2.cloned.1.call-start = ((), (), s32[]{:S(2)}) async-start(), calls=%async_computation.5 | async-start | bytes 4456448 | tf_op jit(solution)/shard_map/all_gather | solution.py:33
  169.3 55.3 %copy-start.3 = (u32[256]{0:T(256)S(1)}, u32[256]{0:T(256)}, u32[]{:S(2)}) copy-start(u32[256]{0:T(256)} %constant.31) | copy-start | bytes 3076
  169.3 47.2 %all-to-all-start = ((bf16[128,16,256]{2,0,1:T(8,128)(2,1)}), bf16[128,16,256]{2,0,1:T(8,128)(2,1)S(1)}, u32[]{:S(2)}, u32[]{:S(2)}) async-start(bf16[128,16,256]{2,0,1:T(8,128)(2,1)} %copy.14), calls=%async_computation | async-start | bytes 2097152 | tf_op jit(solution)/shard_map/all_to_all | solution.py:41
  216.5 65.4 %all-to-all-start.1 = ((bf16[128,16,256]{2,0,1:T(8,128)(2,1)}), bf16[128,16,256]{2,0,1:T(8,128)(2,1)S(1)}, u32[]{:S(2)}, u32[]{:S(2)}) async-start(bf16[128,16,256]{2,0,1:T(8,128)(2,1)} %copy.16), calls=%async_computation.1 | async-start | bytes 2097152 | tf_op jit(solution)/shard_map/all_to_all | solution.py:42
  224.0 169.2 %reduce-scatter.2.cloned.1.call-start = ((), (), s32[]{:S(2)}) async-start(), calls=%async_computation.6 | async-start | bytes 4456448 | tf_op jit(solution)/shard_map/reduce_scatter | solution.py:85
  291.1 102.1 %all-to-all-start.2 = ((bf16[16,128,256]{1,2,0:T(8,128)(2,1)}), bf16[16,128,256]{1,2,0:T(8,128)(2,1)S(1)}, u32[]{:S(2)}, u32[]{:S(2)}) async-start(bf16[16,128,256]{1,2,0:T(8,128)(2,1)} %fusion.3), calls=%async_computation.2 | async-start | bytes 2097152 | tf_op jit(solution)/shard_map/all_to_all | solution.py:83
  294.8 250.1 %all-reduce.6.cloned.1.call-start = ((), (), s32[]{:S(2)}) async-start(), calls=%async_computation.7 | async-start | bytes 524288 | tf_op jit(solution)/shard_map/psum | solution.py:96
  301.7 243.2 %copy-start = (bf16[1,32,4096]{2,1,0:T(8,128)(2,1)S(1)}, bf16[1,32,4096]{2,1,0:T(8,128)(2,1)}, u32[]{:S(2)}) copy-start(bf16[1,32,4096]{2,1,0:T(8,128)(2,1)} %param.7) | copy-start | bytes 786436
  301.7 243.2 %copy-start.2 = (f32[4096]{0:T(1024)S(1)}, f32[4096]{0:T(1024)}, u32[]{:S(2)}) copy-start(f32[4096]{0:T(1024)} %param.8) | copy-start | bytes 49156
Sparse Core Ops, SparseCore 0:
  11.2 155.1 all-reduce.3
  169.1 105.8 all-gather.1
  289.7 103.3 reduce-scatter.1
  395.6 149.2 all-reduce.5
where the time goes:
time: 640 us
  waiting for transfers between devices  439 us (69%)
  blocking collectives  119 us (19%)
  starting transfers between devices  30.4 us (5%)
  matrix products  19.9 us (3%)
  between operations  14.6 us (2%)
  local copies, waits for them, and re-layouts  9.89 us (2%)
  other arithmetic  7.1 us (1%)
    psum x1, waiting for transfers between devices, broadcast(): return lax.psum(block, axis)  156 us
    psum x1, waiting for transfers between devices, on_device(): memory_grad = lax.psum(section_part, 'section').astype(jnp.float32)  150 us
    reduce_scatter x1, waiting for transfers between devices, on_device(): lax.psum_scatter((lax.dot_general(both_grads, w_both, (((1,), (1,)), ((),...  91.4 us
    psum x1, blocking collectives, on_device(): lax.psum(jnp.sum(memory_grad * normed, axis=0) * is_last, ('section', 'dp'))  85.3 us
    unnamed x1, blocking collectives  33.3 us
    all_to_all x1, waiting for transfers between devices, on_device(): lax.all_to_all(queries[0], 'dp', split_axis=1, concat_axis=0, tiled=True)  26.1 us
    all_to_all x1, starting transfers between devices, on_device(): lax.all_to_all(queries[0], 'dp', split_axis=1, concat_axis=0, tiled=True)  19.1 us
    all_gather x1, waiting for transfers between devices, on_device(): lax.all_gather(sent, 'dp', axis=0, tiled=True)  15.6 us
  transfers between devices with their start and end apart: 7, of which 5 were waited for; matrix products, arithmetic and copies ran while one was open for 4% of the time, Pallas kernels for 0%

commit v1 on v0

--- a/solution.py
+++ b/solution.py
@@ -99,7 +99,7 @@
         scaled_grad - normed * jnp.mean(scaled_grad * normed, axis=1, keepdims=True)
     )
     state_grad = (last_grad * is_last).astype(jnp.bfloat16)[None]
-    gain_grad = lax.psum(jnp.sum(memory_grad * normed, axis=0) * is_last, ("section", "dp"))
+    gain_grad = lax.psum(lax.psum(jnp.sum(memory_grad * normed, axis=0) * is_last, "section"), "dp")
     key_weight_grad = weight_grads[:, :local_width][None]
     value_weight_grad = weight_grads[:, local_width:][None]
     return (query_grad, key_weight_grad, value_weight_grad, state_grad, gain_grad)

time: 640 us -> 726 us (1.13)
  blocking collectives: 119 us -> 199 us
    psum x1 -> x2, blocking collectives: 85.3 us -> 166 us  [the longest x1 101 us: on_device(): lax.psum(lax.psum(jnp.sum(memory_grad * normed, axis=0) * is_last, 'secti...]
  transfers between devices with their start and end apart: 7 -> 7, of which waited for: 5 -> 5; matrix products, arithmetic and copies ran while one was open for 4% -> 3% of each run, Pallas kernels for 0% -> 0%
where the time goes in v1:
time: 726 us; the launch traced here: 720 us
  waiting for transfers between devices  439 us (60%)
  blocking collectives  199 us (27%)
  starting transfers between devices  30.4 us (4%)
  matrix products  19.9 us (3%)
  between operations  14.6 us (2%)
  local copies, waits for them, and re-layouts  9.89 us (1%)
    psum x1, waiting for transfers between devices, broadcast(): return lax.psum(block, axis)  156 us
    psum x1, waiting for transfers between devices, on_device(): memory_grad = lax.psum(section_part, 'section').astype(jnp.float32)  150 us
    psum x1, blocking collectives, on_device(): lax.psum(lax.psum(jnp.sum(memory_grad * normed, axis=0) * is_last, 'secti...  101 us
    reduce_scatter x1, waiting for transfers between devices, on_device(): lax.psum_scatter((lax.dot_general(both_grads, w_both, (((1,), (1,)), ((),...  91.4 us
    psum x1, blocking collectives, on_device(): lax.psum(jnp.sum(memory_grad * normed, axis=0) * is_last, 'section')  65.3 us
    unnamed x1, blocking collectives  33.3 us
    all_to_all x1, waiting for transfers between devices, on_device(): lax.all_to_all(queries[0], 'dp', split_axis=1, concat_axis=0, tiled=True)  26.1 us
    all_to_all x1, starting transfers between devices, on_device(): lax.all_to_all(queries[0], 'dp', split_axis=1, concat_axis=0, tiled=True)  19.1 us
  transfers between devices with their start and end apart: 7, of which 5 were waited for; matrix products, arithmetic and copies ran while one was open for 3% of the time, Pallas kernels for 0%

profile of v1, /device:TPU:1, one launch (start us, length us, event | category | flops | bytes accessed | tf_op | source)
XLA Modules:
  0.0 720.4 jit_solution(17861709376003074250)
XLA Ops:
  7.2 1.2 fusion.28
  8.4 1.8 fusion.33
  10.3 156.1 %all-reduce.4.cloned.1.call-done = bf16[32,4096]{1,0:T(8,128)(2,1)} async-done(((bf16[32,4096]{1,0:T(8,128)(2,1)}), bf16[32,4096]{1,0:T(8,128)(2,1)}) %all-reduce.4.cloned.1.call-update) | async-done | bytes 262160 | tf_op jit(solution)/shard_map/psum | solution.py:12
  166.4 1.6 copy.13
  168.0 1.3 copy.14
  169.3 19.1 %all-to-all-start = ((bf16[128,16,256]{2,0,1:T(8,128)(2,1)}), bf16[128,16,256]{2,0,1:T(8,128)(2,1)S(1)}, u32[]{:S(2)}, u32[]{:S(2)}) async-start(bf16[128,16,256]{2,0,1:T(8,128)(2,1)} %copy.14), calls=%async_computation | async-start | bytes 2097152 | tf_op jit(solution)/shard_map/all_to_all | solution.py:41
  188.4 0.7 copy.15
  189.1 1.3 copy.16
  190.4 26.1 %all-to-all-done = bf16[128,16,256]{2,0,1:T(8,128)(2,1)S(1)} async-done(((bf16[128,16,256]{2,0,1:T(8,128)(2,1)}), bf16[128,16,256]{2,0,1:T(8,128)(2,1)S(1)}, u32[]{:S(2)}, u32[]{:S(2)}) %all-to-all-start) | async-done | bytes 1048608 | tf_op jit(solution)/shard_map/all_to_all | solution.py:41
  216.5 7.5 %all-to-all-start.1 = ((bf16[128,16,256]{2,0,1:T(8,128)(2,1)}), bf16[128,16,256]{2,0,1:T(8,128)(2,1)S(1)}, u32[]{:S(2)}, u32[]{:S(2)}) async-start(bf16[128,16,256]{2,0,1:T(8,128)(2,1)} %copy.16), calls=%async_computation.1 | async-start | bytes 2097152 | tf_op jit(solution)/shard_map/all_to_all | solution.py:42
  224.7 0.6 dynamic-slice
  225.3 0.8 dynamic-update-slice
  226.0 33.3 %all-reduce = s32[16]{0:T(128)S(1)} all-reduce(s32[16]{0:T(128)S(1)} %dynamic-update-slice), channel_id=1, replica_groups=mesh['section'=16,'dp'=16] {'dp'}, use_global_device_ids=true, to_apply=%add | all-reduce | flops 16 | bytes 128
  259.4 15.6 %all-gather.2.cloned.1.call-done = bf16[512,4096]{1,0:T(8,128)(2,1)} async-done(((bf16[32,4096]{1,0:T(8,128)(2,1)}), bf16[512,4096]{1,0:T(8,128)(2,1)}) %all-gather.2.cloned.1.call-update) | async-done | bytes 4194320 | tf_op jit(solution)/shard_map/all_gather | solution.py:33
  275.0 5.8 fusion.4
  280.8 0.5 fusion.10
  281.3 0.6 fusion.46
  281.9 0.5 fusion.13
  282.4 0.3 convolution_convert_fusion.1
  282.7 0.3 convolution_convert_fusion.2
  283.0 6.6 multiply_convert_fusion
  289.6 1.5 fusion.3
  291.1 3.7 all-to-all-start.2
  294.8 4.6 multiply_convert_fusion.1
  299.4 2.3 slice_bitcast_fusion
  301.7 91.4 %reduce-scatter.2.cloned.1.call-done = bf16[32,4096]{1,0:T(8,128)(2,1)} async-done(((bf16[512,4096]{1,0:T(8,128)(2,1)}), bf16[32,4096]{1,0:T(8,128)(2,1)}) %reduce-scatter.2.cloned.1.call-update) | async-done | bytes 262160 | tf_op jit(solution)/shard_map/reduce_scatter | solution.py:85
  393.5 1.3 copy.17
  394.8 150.1 %all-reduce.6.cloned.1.call-done = bf16[32,4096]{1,0:T(8,128)(2,1)} async-done(((bf16[32,4096]{1,0:T(8,128)(2,1)}), bf16[32,4096]{1,0:T(8,128)(2,1)}) %all-reduce.6.cloned.1.call-update) | async-done | bytes 262160 | tf_op jit(solution)/shard_map/psum | solution.py:96
  544.9 1.3 fusion.27
  546.2 65.3 %psum.30 = f32[4096]{0:T(1024)S(1)} all-reduce(f32[4096]{0:T(1024)S(1)} %broadcast_multiply_fusion), channel_id=1, replica_groups=mesh['section'=16,'dp'=16] {'section'}, use_global_device_ids=true, to_apply=%region_9.10 | all-reduce | flops 4096 | bytes 32768 | tf_op jit(solution)/shard_map/psum | solution.py:102
  611.4 100.6 %psum.31 = f32[4096]{0:T(1024)} all-reduce(f32[4096]{0:T(1024)S(1)} %psum.30), channel_id=1, replica_groups=mesh['section'=16,'dp'=16] {'dp'}, use_global_device_ids=true, to_apply=%region_10.11 | all-reduce | flops 4096 | bytes 32768 | tf_op jit(solution)/shard_map/psum | solution.py:102
  712.0 1.8 fusion.34
  (25 shorter events, 0.6 us)
Async XLA Ops:
  7.2 181.2 %copy-start.1 = (bf16[1,128,4096]{2,1,0:T(8,128)(2,1)S(1)}, bf16[1,128,4096]{2,1,0:T(8,128)(2,1)}, u32[]{:S(2)}) copy-start(bf16[1,128,4096]{2,1,0:T(8,128)(2,1)} %param.12) | copy-start | bytes 3145732
  7.2 159.2 %all-reduce.4.cloned.1.call-start = ((), (), s32[]{:S(2)}) async-start(), calls=%async_computation.4 | async-start | bytes 524288 | tf_op jit(solution)/shard_map/psum | solution.py:12
  10.3 264.7 %all-gather.2.cloned.1.call-start = ((), (), s32[]{:S(2)}) async-start(), calls=%async_computation.5 | async-start | bytes 4456448 | tf_op jit(solution)/shard_map/all_gather | solution.py:33
  169.3 55.3 %copy-start.3 = (u32[256]{0:T(256)S(1)}, u32[256]{0:T(256)}, u32[]{:S(2)}) copy-start(u32[256]{0:T(256)} %constant.31) | copy-start | bytes 3076
  169.3 47.2 %all-to-all-start = ((bf16[128,16,256]{2,0,1:T(8,128)(2,1)}), bf16[128,16,256]{2,0,1:T(8,128)(2,1)S(1)}, u32[]{:S(2)}, u32[]{:S(2)}) async-start(bf16[128,16,256]{2,0,1:T(8,128)(2,1)} %copy.14), calls=%async_computation | async-start | bytes 2097152 | tf_op jit(solution)/shard_map/all_to_all | solution.py:41
  216.5 65.4 %all-to-all-start.1 = ((bf16[128,16,256]{2,0,1:T(8,128)(2,1)}), bf16[128,16,256]{2,0,1:T(8,128)(2,1)S(1)}, u32[]{:S(2)}, u32[]{:S(2)}) async-start(bf16[128,16,256]{2,0,1:T(8,128)(2,1)} %copy.16), calls=%async_computation.1 | async-start | bytes 2097152 | tf_op jit(solution)/shard_map/all_to_all | solution.py:42
  224.0 169.2 %reduce-scatter.2.cloned.1.call-start = ((), (), s32[]{:S(2)}) async-start(), calls=%async_computation.6 | async-start | bytes 4456448 | tf_op jit(solution)/shard_map/reduce_scatter | solution.py:85
  291.1 102.1 %all-to-all-start.2 = ((bf16[16,128,256]{1,2,0:T(8,128)(2,1)}), bf16[16,128,256]{1,2,0:T(8,128)(2,1)S(1)}, u32[]{:S(2)}, u32[]{:S(2)}) async-start(bf16[16,128,256]{1,2,0:T(8,128)(2,1)} %fusion.3), calls=%async_computation.2 | async-start | bytes 2097152 | tf_op jit(solution)/shard_map/all_to_all | solution.py:83
  294.8 250.1 %all-reduce.6.cloned.1.call-start = ((), (), s32[]{:S(2)}) async-start(), calls=%async_computation.7 | async-start | bytes 524288 | tf_op jit(solution)/shard_map/psum | solution.py:96
  301.7 243.2 %copy-start = (bf16[1,32,4096]{2,1,0:T(8,128)(2,1)S(1)}, bf16[1,32,4096]{2,1,0:T(8,128)(2,1)}, u32[]{:S(2)}) copy-start(bf16[1,32,4096]{2,1,0:T(8,128)(2,1)} %param.7) | copy-start | bytes 786436
  301.7 243.2 %copy-start.2 = (f32[4096]{0:T(1024)S(1)}, f32[4096]{0:T(1024)}, u32[]{:S(2)}) copy-start(f32[4096]{0:T(1024)} %param.8) | copy-start | bytes 49156
Sparse Core Ops, SparseCore 0:
  11.2 155.1 all-reduce.3
  169.1 105.8 all-gather.1
  289.7 103.3 reduce-scatter.1
  395.6 149.2 all-reduce.5
